TPU v7x, 32 devices: a whole 2x2x4 slice. The times are simulated.
32 devices in a mesh: groups: 2 (over x), dap: 16 (over z, y, core).
Axes of the slice: x: 2, y: 2, z: 4, core: 2. Of those that a mesh axis runs over, the one named last changes fastest.
Arguments:
- homolog_tensor: bfloat16 [128, 32, 256], P(('groups', 'dap')), parts along dimension 0, may hold values from -1 to 1
- couple_tensor: bfloat16 [64, 32, 128], P(('groups', 'dap')), parts along dimension 0, may hold values from -6 to 6
- horizontal_drop_filter: int32 [64, 256], P('groups'), parts along dimension 0, may hold values 0 or 1
- couple_offset_matrix: bfloat16 [128, 8], replicated, may hold values from -0.29882812 to 0.29882812
- horizontal_attend_matrix: bfloat16 [256, 1024], replicated, may hold values from -0.375 to 0.375
- horizontal_exit_matrix: bfloat16 [256, 256], replicated, may hold values from -0.375 to 0.375
- vertical_attend_matrix: bfloat16 [256, 1024], replicated, may hold values from -0.375 to 0.375
- vertical_exit_matrix: bfloat16 [256, 256], replicated, may hold values from -0.375 to 0.375
- averaged_product_flanks: bfloat16 [256, 64], replicated, may hold values from -0.375 to 0.375
- averaged_product_exit: bfloat16 [1024, 128], replicated, may hold values from -1 to 1
Outputs:
- alignment_output: bfloat16 [128, 32, 256], P('groups', 'dap'), parts along dimension 0
- pair_output_state: bfloat16 [64, 32, 128], P(('groups', 'dap')), parts along dimension 0
There are 2 independent parts, one for each index of `groups`. A program takes and returns all parts, laid end to end along the dimension named above; an argument that names none is the same for every part. Nothing has to cross between parts.
All inputs are finite; a program needn't handle non-finite values.
Results may differ from a plain program's by a relative error of at most 0.012.
Values may be sent and summed in bfloat16 or wider, within the bound.
No kernel may reach another device: no remote copies, remote signals or barrier semaphores. Data moves between devices by JAX's collectives and lax.ppermute only.
A program may use at most 64 MiB of HBM per device.

v0:
```python
import jax
import jax.numpy as jnp
from jax import lax
from jax.sharding import PartitionSpec as P

HEAD_NUMBER = 8
HEAD_WIDTH = 32
FACTOR_FEATURES = 32


def standardise_features(values):
    values = values.astype(jnp.float32)
    center = values - jnp.mean(values, axis=-1, keepdims=True)
    spread = jnp.mean(center * center, axis=-1, keepdims=True)
    return center * lax.rsqrt(spread + 1e-05)


def attend(normed, w_qkvg, w_out, bias):
    batch, length = (normed.shape[0], normed.shape[1])
    proj = jnp.einsum("blc,cf->blf", normed, w_qkvg, preferred_element_type=jnp.float32)
    proj = proj.reshape(batch, length, 4, HEAD_NUMBER, HEAD_WIDTH)
    query = (proj[:, :, 0] * HEAD_WIDTH ** (-0.5)).astype(jnp.bfloat16)
    keys = proj[:, :, 1].astype(jnp.bfloat16)
    values = proj[:, :, 2].astype(jnp.bfloat16)
    gate = proj[:, :, 3]
    if bias is None:
        bias = jnp.zeros((HEAD_NUMBER, length, length), jnp.bfloat16)

    def one_head(items):
        qh, kh, vh, bh = items
        scores = jnp.einsum("bid,bjd->bij", qh, kh, preferred_element_type=jnp.float32)
        scores = scores + bh.astype(jnp.float32)[None]
        weights = jax.nn.softmax(scores, axis=-1).astype(jnp.bfloat16)
        return jnp.einsum("bij,bjd->bid", weights, vh, preferred_element_type=jnp.float32)

    heads = lax.map(
        one_head,
        (jnp.moveaxis(query, 2, 0), jnp.moveaxis(keys, 2, 0), jnp.moveaxis(values, 2, 0), bias),
    )
    heads = jnp.moveaxis(heads, 0, 2)
    gated = (
        (jax.nn.sigmoid(gate) * heads)
        .astype(jnp.bfloat16)
        .reshape(batch, length, HEAD_NUMBER * HEAD_WIDTH)
    )
    return jnp.einsum("blk,kc->blc", gated, w_out, preferred_element_type=jnp.float32)


def shards(
    homolog_tensor,
    couple_tensor,
    horizontal_drop_filter,
    couple_offset_matrix,
    horizontal_attend_matrix,
    horizontal_exit_matrix,
    vertical_attend_matrix,
    vertical_exit_matrix,
    averaged_product_flanks,
    averaged_product_exit,
):
    normed_pair = standardise_features(couple_tensor).astype(jnp.bfloat16)
    own_bias = jnp.einsum(
        "ijz,zh->hij", normed_pair, couple_offset_matrix, preferred_element_type=jnp.float32
    ).astype(jnp.bfloat16)
    bias = lax.all_gather(own_bias, "dap", axis=1, tiled=True)
    starting_answer = standardise_features(homolog_tensor).astype(jnp.bfloat16)
    perform_refresh = attend(
        starting_answer, horizontal_attend_matrix, horizontal_exit_matrix, bias
    )
    homolog_later = (
        homolog_tensor.astype(jnp.float32)
        + horizontal_drop_filter.astype(jnp.float32) * (1.0 / 0.9) * perform_refresh
    ).astype(jnp.bfloat16)
    incoming_blocks = lax.all_to_all(homolog_later, "dap", split_axis=1, concat_axis=0, tiled=True)
    column_layout = jnp.swapaxes(incoming_blocks, 0, 1)
    perform_refresh = attend(
        standardise_features(column_layout).astype(jnp.bfloat16),
        vertical_attend_matrix,
        vertical_exit_matrix,
        None,
    )
    alignment_output = jnp.swapaxes(
        (column_layout.astype(jnp.float32) + perform_refresh).astype(jnp.bfloat16), 0, 1
    )
    final_result = standardise_features(alignment_output).astype(jnp.bfloat16)
    factors = jnp.einsum(
        "sic,cf->sif", final_result, averaged_product_flanks, preferred_element_type=jnp.float32
    )
    left = factors[..., :FACTOR_FEATURES].astype(jnp.bfloat16)
    right = factors[..., FACTOR_FEATURES:].astype(jnp.bfloat16)
    total = left.shape[0]
    own_rows = left.shape[1]
    whole = lax.all_gather(right, "dap", axis=1, tiled=True)
    outer = jnp.einsum("sic,sjd->ijcd", left, whole, preferred_element_type=jnp.float32) / total
    outer = outer.astype(jnp.bfloat16).reshape(
        own_rows, whole.shape[1], FACTOR_FEATURES * FACTOR_FEATURES
    )
    change = jnp.einsum(
        "ijk,kz->ijz", outer, averaged_product_exit, preferred_element_type=jnp.float32
    )
    pair_output_state = (couple_tensor.astype(jnp.float32) + change).astype(jnp.bfloat16)
    return (alignment_output, pair_output_state)


def solution(mesh):
    placed = (
        P(("groups", "dap"), None, None),
        P(("groups", "dap"), None, None),
        P("groups", None),
        P(),
        P(),
        P(),
        P(),
        P(),
        P(),
        P(),
    )
    return jax.shard_map(
        shards,
        mesh=mesh,
        in_specs=placed,
        out_specs=(P("groups", "dap", None), P(("groups", "dap"), None, None)),
        check_vma=False,
    )
```

profile of v0, /device:TPU:0, one launch (start us, length us, event | category | flops | bytes accessed | tf_op | source)
XLA Modules:
  0.0 80.2 jit_solution(14656866743398978957)
XLA Ops:
  0.6 1.0 %convert_reduce_fusion = f32[4,32]{1,0:T(4,128)S(1)} fusion(bf16[4,32,256]{2,1,0:T(8,128)(2,1)} %param.14), kind=kLoop, calls=%fused_computation.81 | loop fusion | flops 65408 | bytes 66048 | tf_op jit(solution)/shard_map/reduce_sum | solution.py:13
  1.7 1.0 %fusion.104 = f32[4,32]{1,0:T(4,128)S(1)} fusion(bf16[4,32,256]{2,1,0:T(8,128)(2,1)} %param.14, f32[4,32]{1,0:T(4,128)S(1)} %broadcast_multiply_fusion), kind=kLoop, calls=%fused_computation.88 | loop fusion | flops 130944 | bytes 66560 | tf_op jit(solution)/shard_map/reduce_sum | solution.py:14
  2.7 1.1 %fusion.87 = f32[4,32,1024]{2,1,0:T(8,128)S(1)} fusion(bf16[256,1024]{1,0:T(8,128)(2,1)S(1)} %copy-done, bf16[4,32,256]{2,1,0:T(8,128)(2,1)} %param.14, f32[4,32]{1,0:T(4,128)S(1)} %add_rsqrt_fusion, f32[4,32]{1,0:T(4,128)S(1)} %broadcast_multiply_fusion), kind=kOutput, calls=%fused_computation.63 | convolution fusion | flops 67239936 | bytes 1115136 | tf_op jit(solution)/shard_map/blc,cf->blf/dot_general | solution.py:20
  3.8 0.7 reshape.102
  4.5 2.6 %copy.41 = f32[4,32,4,8,32]{4,1,0,3,2:T(8,128)} copy(f32[4,32,4,8,32]{4,3,2,1,0:T(8,128)S(1)} %reshape.102) | data formatting | bytes 1048576 | tf_op jit(solution)/shard_map/reshape | solution.py:21
  7.1 2.2 %copy.76 = bf16[4,32,4,8,32]{4,1,0,3,2:T(8,128)(2,1)} copy(f32[4,32,4,8,32]{4,3,2,1,0:T(8,128)S(1)} %reshape.102) | data formatting | bytes 786432 | tf_op jit(solution)/shard_map/reshape | solution.py:21
  9.3 1.1 %fusion.90 = bf16[8,4,32,32]{3,2,1,0:T(8,128)(2,1)S(1)} fusion(f32[4,32,4,8,32]{4,1,0,3,2:T(8,128)} %copy.41), kind=kLoop, calls=%fused_computation.66 | loop fusion | flops 65536 | bytes 196608 | tf_op jit(solution)/shard_map/transpose | solution.py:38
  10.4 1.1 %slice_bitcast_fusion = (bf16[8,4,32,32]{3,2,1,0:T(8,128)(2,1)S(1)}, bf16[8,4,32,32]{3,2,1,0:T(8,128)(2,1)S(1)}) fusion(bf16[4,32,4,8,32]{4,1,0,3,2:T(8,128)(2,1)} %copy.76), kind=kLoop, calls=%fused_computation.75 | loop fusion | bytes 262144 | tf_op jit(solution)/shard_map/transpose | solution.py:38
  11.9 23.3 %all_gather.6 = bf16[8,32,32]{2,0,1:T(8,128)(2,1)S(1)} all-gather(bf16[8,2,32]{2,0,1:T(8,128)(2,1)S(1)} %fusion.78), channel_id=1, replica_groups=mesh['groups'=2,'dap'=16] {'dap'}, dimensions={1}, use_global_device_ids=true | all-gather | bytes 17408 | tf_op jit(solution)/shard_map/all_gather | solution.py:65
  35.4 4.3 %while.20 = (s32[]{:T(128)}, f32[8,4,32,32]{3,2,1,0:T(8,128)S(1)}, bf16[8,4,32,32]{3,2,1,0:T(8,128)(2,1)S(1)}, bf16[8,4,32,32]{3,2,1,0:T(8,128)(2,1)S(1)}, bf16[...) while((s32[]{:T(128)}, f32[8,4,32,32]{3,2,1,0:T(8,128)S(1)}, ...), condition=%wide.region_7.8_spmd, body=%wide.region_4.7_spmd.sunk | while | flops 816320 | bytes 274001 | solution.py:36
  35.6 0.3 fusion.162
  36.1 0.3 fusion.162
  38.8 0.3 fusion.162
  39.3 0.3 fusion.162
  39.7 1.3 %fusion.89 = bf16[4,32,8,32]{3,1,0,2:T(8,128)(2,1)S(1)} fusion(f32[8,4,32,32]{3,2,1,0:T(8,128)S(1)} %get-tuple-element.61, f32[4,32,4,8,32]{4,1,0,3,2:T(8,128)} %copy.41), kind=kLoop, calls=%fused_computation.65 | loop fusion | flops 163840 | bytes 327680 | tf_op jit(solution)/shard_map/convert_element_type | solution.py:43
  41.5 0.7 copy.46
  42.2 3.5 %all-to-all-start = ((bf16[4,32,256]{2,0,1:T(4,128)(2,1)}), bf16[4,32,256]{2,0,1:T(4,128)(2,1)S(1)}, u32[]{:S(2)}, u32[]{:S(2)}) async-start(bf16[4,32,256]{2,0,1:T(4,128)(2,1)} %copy.46), calls=%async_computation | async-start | bytes 131072 | tf_op jit(solution)/shard_map/all_to_all | solution.py:74
  45.7 6.8 %all-to-all-done = bf16[4,32,256]{2,0,1:T(4,128)(2,1)S(1)} async-done(((bf16[4,32,256]{2,0,1:T(4,128)(2,1)}), bf16[4,32,256]{2,0,1:T(4,128)(2,1)S(1)}, u32[]{:S(2)}, u32[]{:S(2)}) %all-to-all-start) | async-done | bytes 65568 | tf_op jit(solution)/shard_map/all_to_all | solution.py:74
  52.9 0.4 fusion.85
  53.5 4.7 %while.21 = (s32[]{:T(128)}, f32[8,2,64,32]{2,3,0,1:T(8,128)S(1)}, bf16[8,2,64,32]{2,3,0,1:T(8,128)(2,1)S(1)}, bf16[8,2,64,32]{2,3,0,1:T(8,128)(2,1)S(1)}, bf16[8,2,64,32]{2,3,0,1:T(8,128)(2,1)S(1)}, /*index=5*/s32[]{:T(128)}) while((s32[]{:T(128)}, f32[8,2,64,32]{2,3,0,1:T(8,128)S(1)}, bf16[8,2,64,32]{2,3,0,1:T(8,128)(2,1)S(1)}, ...), condition=%wide.region_13.14_spmd, body=%wide.region_10.13_spmd.sunk | while | flops 1614080 | bytes 119365 | solution.py:36
  53.8 0.3 fusion.169
  54.4 0.3 fusion.169
  55.0 0.3 fusion.169
  55.6 0.3 fusion.169
  56.1 0.3 fusion.169
  56.7 0.3 fusion.169
  57.3 0.3 fusion.169
  57.9 0.3 fusion.169
  58.7 0.7 copy.55
  59.8 18.5 %all_gather.7 = bf16[64,32,32]{0,2,1:T(8,128)(2,1)S(1)} all-gather(bf16[64,2,32]{0,2,1:T(8,128)(2,1)S(1)} %slice.54), channel_id=1, replica_groups=mesh['groups'=2,'dap'=16] {'dap'}, dimensions={1}, use_global_device_ids=true | all-gather | bytes 139264 | tf_op jit(solution)/shard_map/all_gather | solution.py:93
  78.9 0.5 reshape.106
  79.5 0.8 fusion.77
  (80 shorter events, 7.8 us)
Async XLA Ops:
  0.6 2.0 %copy-start = (bf16[256,1024]{1,0:T(8,128)(2,1)S(1)}, bf16[256,1024]{1,0:T(8,128)(2,1)}, u32[]{:S(2)}) copy-start(bf16[256,1024]{1,0:T(8,128)(2,1)} %param.18) | copy-start | bytes 1572868
  7.1 4.4 %copy-start.4 = (bf16[2,32,128]{2,1,0:T(8,128)(2,1)S(1)}, bf16[2,32,128]{2,1,0:T(8,128)(2,1)}, u32[]{:S(2)}) copy-start(bf16[2,32,128]{2,1,0:T(8,128)(2,1)} %param.15) | copy-start | bytes 49156
  7.1 4.7 %copy-start.9 = (bf16[128,8]{0,1:T(8,128)(2,1)S(1)}, bf16[128,8]{0,1:T(8,128)(2,1)}, u32[]{:S(2)}) copy-start(bf16[128,8]{0,1:T(8,128)(2,1)} %param.17) | copy-start | bytes 6148
  35.4 5.9 %copy-start.7 = (s32[32,256]{1,0:T(8,128)S(1)}, s32[32,256]{1,0:T(8,128)}, u32[]{:S(2)}) copy-start(s32[32,256]{1,0:T(8,128)} %param.16) | copy-start | bytes 98308
  35.4 5.9 %copy-start.1 = (bf16[4,32,256]{2,1,0:T(8,128)(2,1)S(1)}, bf16[4,32,256]{2,1,0:T(8,128)(2,1)}, u32[]{:S(2)}) copy-start(bf16[4,32,256]{2,1,0:T(8,128)(2,1)} %param.14) | copy-start | bytes 196612
  35.4 5.9 %copy-start.6 = (bf16[256,256]{1,0:T(8,128)(2,1)S(1)}, bf16[256,256]{1,0:T(8,128)(2,1)}, u32[]{:S(2)}) copy-start(bf16[256,256]{1,0:T(8,128)(2,1)} %param.19) | copy-start | bytes 393220
  39.7 13.2 %copy-start.2 = (bf16[256,1024]{1,0:T(8,128)(2,1)S(1)}, bf16[256,1024]{1,0:T(8,128)(2,1)}, u32[]{:S(2)}) copy-start(bf16[256,1024]{1,0:T(8,128)(2,1)} %param.20) | copy-start | bytes 1572868
  42.2 10.4 %all-to-all-start = ((bf16[4,32,256]{2,0,1:T(4,128)(2,1)}), bf16[4,32,256]{2,0,1:T(4,128)(2,1)S(1)}, u32[]{:S(2)}, u32[]{:S(2)}) async-start(bf16[4,32,256]{2,0,1:T(4,128)(2,1)} %copy.46), calls=%async_computation | async-start | bytes 131072 | tf_op jit(solution)/shard_map/all_to_all | solution.py:74
  53.4 4.9 %copy-start.5 = (bf16[256,256]{1,0:T(8,128)(2,1)S(1)}, bf16[256,256]{1,0:T(8,128)(2,1)}, u32[]{:S(2)}) copy-start(bf16[256,256]{1,0:T(8,128)(2,1)} %param.21) | copy-start | bytes 393220
  53.5 6.1 %copy-start.8 = (bf16[256,64]{0,1:T(8,128)(2,1)S(1)}, bf16[256,64]{0,1:T(8,128)(2,1)}, u32[]{:S(2)}) copy-start(bf16[256,64]{0,1:T(8,128)(2,1)} %param.22) | copy-start | bytes 98308
  58.3 21.2 %copy-start.3 = (bf16[1024,128]{1,0:T(8,128)(2,1)S(1)}, bf16[1024,128]{1,0:T(8,128)(2,1)}, u32[]{:S(2)}) copy-start(bf16[1024,128]{1,0:T(8,128)(2,1)} %param.23) | copy-start | bytes 786436
where the time goes:
time: 80.6 us; the launch traced here: 80.2 us
  blocking collectives  41.8 us (52%)
  matrix products  12.4 us (15%)
  local copies, waits for them, and re-layouts  9.33 us (12%)
  waiting for transfers between devices  6.85 us (8%)
  other arithmetic  5.33 us (7%)
  starting transfers between devices  3.5 us (4%)
  between operations  0.95 us (1%)
    all_gather x1, blocking collectives, shards(): bias = lax.all_gather(own_bias, 'dap', axis=1, tiled=True)  23.3 us
    all_gather x1, blocking collectives, shards(): whole = lax.all_gather(right, 'dap', axis=1, tiled=True)  18.5 us
    all_to_all x1, waiting for transfers between devices, shards(): lax.all_to_all(homolog_later, 'dap', split_axis=1, concat_axis=0, tiled=T...  6.85 us
    dot_general x16, matrix products, one_head(): jnp.einsum('bij,bjd->bid', weights, vh, preferred_element_type=jnp.float32)  5.53 us
    reshape x3, local copies, waits for them, and re-layouts, attend(): proj = proj.reshape(batch, length, 4, HEAD_NUMBER, HEAD_WIDTH)  5.46 us
    all_to_all x1, starting transfers between devices, shards(): lax.all_to_all(homolog_later, 'dap', split_axis=1, concat_axis=0, tiled=T...  3.5 us
    sub x16, matrix products, one_head(): weights = jax.nn.softmax(scores, axis=-1).astype(jnp.bfloat16)  3.4 us
  transfers between devices with their start and end apart: 1, of which 1 were waited for; matrix products, arithmetic and copies ran while one was open for 0% of the time, Pallas kernels for 0%

commit v1 on v0

--- a/solution.py
+++ b/solution.py
@@ -71,7 +71,12 @@
         homolog_tensor.astype(jnp.float32)
         + horizontal_drop_filter.astype(jnp.float32) * (1.0 / 0.9) * perform_refresh
     ).astype(jnp.bfloat16)
-    incoming_blocks = lax.all_to_all(homolog_later, "dap", split_axis=1, concat_axis=0, tiled=True)
+    incoming_blocks = jnp.concatenate(
+        lax.all_to_all(
+            jnp.stack(jnp.split(homolog_later, lax.axis_size("dap"), axis=1)), "dap", 0, 0
+        ),
+        axis=0,
+    )
     column_layout = jnp.swapaxes(incoming_blocks, 0, 1)
     perform_refresh = attend(
         standardise_features(column_layout).astype(jnp.bfloat16),

time: 80.6 us -> 89.4 us (1.11)
  local copies, waits for them, and re-layouts: 9.33 us -> 18.2 us
    unnamed x21 -> x36, local copies, waits for them, and re-layouts: 0.76 us -> 9.74 us
where the time goes in v1:
time: 89.4 us; the launch traced here: 89 us
  blocking collectives  41.7 us (47%)
  local copies, waits for them, and re-layouts  18.2 us (20%)
  matrix products  12.4 us (14%)
  waiting for transfers between devices  6.85 us (8%)
  other arithmetic  5.36 us (6%)
  starting transfers between devices  3.5 us (4%)
  between operations  0.95 us (1%)
    all_gather x1, blocking collectives, shards(): bias = lax.all_gather(own_bias, 'dap', axis=1, tiled=True)  23.3 us
    all_gather x1, blocking collectives, shards(): whole = lax.all_gather(right, 'dap', axis=1, tiled=True)  18.4 us
    unnamed x36, local copies, waits for them, and re-layouts  9.74 us
    all_to_all x1, waiting for transfers between devices, shards(): lax.all_to_all(jnp.stack(jnp.split(homolog_later, lax.axis_size('dap'), a...  6.85 us
    dot_general x16, matrix products, one_head(): jnp.einsum('bij,bjd->bid', weights, vh, preferred_element_type=jnp.float32)  5.53 us
    reshape x3, local copies, waits for them, and re-layouts, attend(): proj = proj.reshape(batch, length, 4, HEAD_NUMBER, HEAD_WIDTH)  5.46 us
    all_to_all x1, starting transfers between devices, shards(): lax.all_to_all(jnp.stack(jnp.split(homolog_later, lax.axis_size('dap'), a...  3.5 us
    sub x16, matrix products, one_head(): weights = jax.nn.softmax(scores, axis=-1).astype(jnp.bfloat16)  3.4 us
  transfers between devices with their start and end apart: 1, of which 1 were waited for; matrix products, arithmetic and copies ran while one was open for 0% of the time, Pallas kernels for 0%

profile of v1, /device:TPU:0, one launch (start us, length us, event | category | flops | bytes accessed | tf_op | source)
XLA Modules:
  0.0 89.0 jit_solution(15391860364701758695)
XLA Ops:
  0.6 1.0 %convert_reduce_fusion = f32[4,32]{1,0:T(4,128)S(1)} fusion(bf16[4,32,256]{2,1,0:T(8,128)(2,1)} %param.14), kind=kLoop, calls=%fused_computation.81 | loop fusion | flops 65408 | bytes 66048 | tf_op jit(solution)/shard_map/reduce_sum | solution.py:13
  1.7 1.0 %fusion.104 = f32[4,32]{1,0:T(4,128)S(1)} fusion(bf16[4,32,256]{2,1,0:T(8,128)(2,1)} %param.14, f32[4,32]{1,0:T(4,128)S(1)} %broadcast_multiply_fusion), kind=kLoop, calls=%fused_computation.88 | loop fusion | flops 130944 | bytes 66560 | tf_op jit(solution)/shard_map/reduce_sum | solution.py:14
  2.7 1.1 %fusion.87 = f32[4,32,1024]{2,1,0:T(8,128)S(1)} fusion(bf16[256,1024]{1,0:T(8,128)(2,1)S(1)} %copy-done, bf16[4,32,256]{2,1,0:T(8,128)(2,1)} %param.14, f32[4,32]{1,0:T(4,128)S(1)} %add_rsqrt_fusion, f32[4,32]{1,0:T(4,128)S(1)} %broadcast_multiply_fusion), kind=kOutput, calls=%fused_computation.63 | convolution fusion | flops 67239936 | bytes 1115136 | tf_op jit(solution)/shard_map/blc,cf->blf/dot_general | solution.py:20
  3.8 0.7 reshape.99
  4.5 2.6 %copy.43 = f32[4,32,4,8,32]{4,1,0,3,2:T(8,128)} copy(f32[4,32,4,8,32]{4,3,2,1,0:T(8,128)S(1)} %reshape.99) | data formatting | bytes 1048576 | tf_op jit(solution)/shard_map/reshape | solution.py:21
  7.1 2.2 %copy.82 = bf16[4,32,4,8,32]{4,1,0,3,2:T(8,128)(2,1)} copy(f32[4,32,4,8,32]{4,3,2,1,0:T(8,128)S(1)} %reshape.99) | data formatting | bytes 786432 | tf_op jit(solution)/shard_map/reshape | solution.py:21
  9.3 1.1 %fusion.90 = bf16[8,4,32,32]{3,2,1,0:T(8,128)(2,1)S(1)} fusion(f32[4,32,4,8,32]{4,1,0,3,2:T(8,128)} %copy.43), kind=kLoop, calls=%fused_computation.66 | loop fusion | flops 65536 | bytes 196608 | tf_op jit(solution)/shard_map/transpose | solution.py:38
  10.4 1.1 %slice_bitcast_fusion = (bf16[8,4,32,32]{3,2,1,0:T(8,128)(2,1)S(1)}, bf16[8,4,32,32]{3,2,1,0:T(8,128)(2,1)S(1)}) fusion(bf16[4,32,4,8,32]{4,1,0,3,2:T(8,128)(2,1)} %copy.82), kind=kLoop, calls=%fused_computation.75 | loop fusion | bytes 262144 | tf_op jit(solution)/shard_map/transpose | solution.py:38
  11.9 23.3 %all_gather.6 = bf16[8,32,32]{2,0,1:T(8,128)(2,1)S(1)} all-gather(bf16[8,2,32]{2,0,1:T(8,128)(2,1)S(1)} %fusion.78), channel_id=1, replica_groups=mesh['groups'=2,'dap'=16] {'dap'}, dimensions={1}, use_global_device_ids=true | all-gather | bytes 17408 | tf_op jit(solution)/shard_map/all_gather | solution.py:65
  35.4 4.3 %while.20 = (s32[]{:T(128)}, f32[8,4,32,32]{3,2,1,0:T(8,128)S(1)}, bf16[8,4,32,32]{3,2,1,0:T(8,128)(2,1)S(1)}, bf16[8,4,32,32]{3,2,1,0:T(8,128)(2,1)S(1)}, bf16[...) while((s32[]{:T(128)}, f32[8,4,32,32]{3,2,1,0:T(8,128)S(1)}, ...), condition=%wide.region_7.8_spmd, body=%wide.region_4.7_spmd.sunk | while | flops 816320 | bytes 274001 | solution.py:36
  39.7 1.3 %fusion.89 = bf16[4,32,8,32]{3,1,0,2:T(8,128)(2,1)S(1)} fusion(f32[8,4,32,32]{3,2,1,0:T(8,128)S(1)} %get-tuple-element.61, f32[4,32,4,8,32]{4,1,0,3,2:T(8,128)} %copy.43), kind=kLoop, calls=%fused_computation.65 | loop fusion | flops 163840 | bytes 327680 | tf_op jit(solution)/shard_map/convert_element_type | solution.py:43
  41.5 0.6 constant_dynamic-update-slice_fusion.15
  42.1 0.6 constant_dynamic-update-slice_fusion.14
  42.7 0.6 constant_dynamic-update-slice_fusion.13
  43.3 0.6 constant_dynamic-update-slice_fusion.12
  43.9 0.6 constant_dynamic-update-slice_fusion.11
  44.5 0.6 constant_dynamic-update-slice_fusion.10
  45.1 0.6 constant_dynamic-update-slice_fusion.9
  45.7 0.6 constant_dynamic-update-slice_fusion.8
  46.3 0.6 constant_dynamic-update-slice_fusion.7
  46.9 0.6 constant_dynamic-update-slice_fusion.6
  47.5 0.6 constant_dynamic-update-slice_fusion.5
  48.1 0.6 constant_dynamic-update-slice_fusion.4
  49.3 0.6 constant_dynamic-update-slice_fusion.2
  49.9 0.6 constant_dynamic-update-slice_fusion.1
  50.5 0.6 constant_dynamic-update-slice_fusion
  51.1 3.5 %all-to-all-start = ((bf16[16,4,2,256]{3,2,1,0:T(2,128)(2,1)}), bf16[16,4,2,256]{3,2,1,0:T(2,128)(2,1)S(1)}, u32[]{:S(2)}, u32[]{:S(2)}) async-start(bf16[16,4,2,256]{3,2,1,0:T(2,128)(2,1)} %constant_dynamic-update-slice_fusion), calls=%async_computation | async-start | bytes 131072 | tf_op jit(solution)/shard_map/all_to_all | solution.py:75
  54.6 6.8 %all-to-all-done = bf16[16,4,2,256]{3,2,1,0:T(2,128)(2,1)S(1)} async-done(((bf16[16,4,2,256]{3,2,1,0:T(2,128)(2,1)}), bf16[16,4,2,256]{3,2,1,0:T(2,128)(2,1)S(1)}, u32[]{:S(2)}, u32[]{:S(2)}) %all-to-all-start) | async-done | bytes 65568 | tf_op jit(solution)/shard_map/all_to_all | solution.py:75
  62.4 4.7 %while.21 = (s32[]{:T(128)}, f32[8,2,64,32]{2,3,0,1:T(8,128)S(1)}, bf16[8,2,64,32]{2,3,0,1:T(8,128)(2,1)S(1)}, bf16[8,2,64,32]{2,3,0,1:T(8,128)(2,1)S(1)}, bf16[8,2,64,32]{2,3,0,1:T(8,128)(2,1)S(1)}, /*index=5*/s32[]{:T(128)}) while((s32[]{:T(128)}, f32[8,2,64,32]{2,3,0,1:T(8,128)S(1)}, bf16[8,2,64,32]{2,3,0,1:T(8,128)(2,1)S(1)}, ...), condition=%wide.region_13.14_spmd, body=%wide.region_10.13_spmd.sunk | while | flops 1614080 | bytes 119365 | solution.py:36
  67.6 0.7 copy.57
  68.7 18.4 %all_gather.7 = bf16[64,32,32]{0,2,1:T(8,128)(2,1)S(1)} all-gather(bf16[64,2,32]{0,2,1:T(8,128)(2,1)S(1)} %slice.54), channel_id=1, replica_groups=mesh['groups'=2,'dap'=16] {'dap'}, dimensions={1}, use_global_device_ids=true | all-gather | bytes 139264 | tf_op jit(solution)/shard_map/all_gather | solution.py:98
  88.3 0.8 fusion.77
  (94 shorter events, 13.5 us)
Async XLA Ops:
  0.6 2.0 %copy-start = (bf16[256,1024]{1,0:T(8,128)(2,1)S(1)}, bf16[256,1024]{1,0:T(8,128)(2,1)}, u32[]{:S(2)}) copy-start(bf16[256,1024]{1,0:T(8,128)(2,1)} %param.18) | copy-start | bytes 1572868
  7.1 4.4 %copy-start.4 = (bf16[2,32,128]{2,1,0:T(8,128)(2,1)S(1)}, bf16[2,32,128]{2,1,0:T(8,128)(2,1)}, u32[]{:S(2)}) copy-start(bf16[2,32,128]{2,1,0:T(8,128)(2,1)} %param.15) | copy-start | bytes 49156
  7.1 4.7 %copy-start.9 = (bf16[128,8]{0,1:T(8,128)(2,1)S(1)}, bf16[128,8]{0,1:T(8,128)(2,1)}, u32[]{:S(2)}) copy-start(bf16[128,8]{0,1:T(8,128)(2,1)} %param.17) | copy-start | bytes 6148
  35.4 5.9 %copy-start.7 = (s32[32,256]{1,0:T(8,128)S(1)}, s32[32,256]{1,0:T(8,128)}, u32[]{:S(2)}) copy-start(s32[32,256]{1,0:T(8,128)} %param.16) | copy-start | bytes 98308
  35.4 5.9 %copy-start.1 = (bf16[4,32,256]{2,1,0:T(8,128)(2,1)S(1)}, bf16[4,32,256]{2,1,0:T(8,128)(2,1)}, u32[]{:S(2)}) copy-start(bf16[4,32,256]{2,1,0:T(8,128)(2,1)} %param.14) | copy-start | bytes 196612
  35.4 5.9 %copy-start.6 = (bf16[256,256]{1,0:T(8,128)(2,1)S(1)}, bf16[256,256]{1,0:T(8,128)(2,1)}, u32[]{:S(2)}) copy-start(bf16[256,256]{1,0:T(8,128)(2,1)} %param.19) | copy-start | bytes 393220
  39.7 22.1 %copy-start.2 = (bf16[256,1024]{1,0:T(8,128)(2,1)S(1)}, bf16[256,1024]{1,0:T(8,128)(2,1)}, u32[]{:S(2)}) copy-start(bf16[256,1024]{1,0:T(8,128)(2,1)} %param.20) | copy-start | bytes 1572868
  51.1 10.4 %all-to-all-start = ((bf16[16,4,2,256]{3,2,1,0:T(2,128)(2,1)}), bf16[16,4,2,256]{3,2,1,0:T(2,128)(2,1)S(1)}, u32[]{:S(2)}, u32[]{:S(2)}) async-start(bf16[16,4,2,256]{3,2,1,0:T(2,128)(2,1)} %constant_dynamic-update-slice_fusion), calls=%async_computation | async-start | bytes 131072 | tf_op jit(solution)/shard_map/all_to_all | solution.py:75
  62.3 4.9 %copy-start.5 = (bf16[256,256]{1,0:T(8,128)(2,1)S(1)}, bf16[256,256]{1,0:T(8,128)(2,1)}, u32[]{:S(2)}) copy-start(bf16[256,256]{1,0:T(8,128)(2,1)} %param.21) | copy-start | bytes 393220
  62.4 6.1 %copy-start.8 = (bf16[256,64]{0,1:T(8,128)(2,1)S(1)}, bf16[256,64]{0,1:T(8,128)(2,1)}, u32[]{:S(2)}) copy-start(bf16[256,64]{0,1:T(8,128)(2,1)} %param.22) | copy-start | bytes 98308
  67.2 21.1 %copy-start.3 = (bf16[1024,128]{1,0:T(8,128)(2,1)S(1)}, bf16[1024,128]{1,0:T(8,128)(2,1)}, u32[]{:S(2)}) copy-start(bf16[1024,128]{1,0:T(8,128)(2,1)} %param.23) | copy-start | bytes 786436
